TPU v7x, 256 devices: a whole 4x4x8 slice. The times are simulated.
256 devices in a mesh: ckpt: 4 (over z_lo), tok: 64 (over y, z_hi, x, core).
Axes of the slice: x: 4, y: 4, z: 8 (z_hi: 2, z_lo: 4; z = z_hi * 4 + z_lo), core: 2. Of those that a mesh axis runs over, the one named last changes fastest.
Arguments:
- features: bfloat16 [4, 8192, 1792], P('ckpt', 'tok'), may hold values from -22 to 22
- pairing: int32 [4, 64, 128], P('ckpt', 'tok'), may hold values from 0 to 127, each once within a row
- rotation: bfloat16 [4, 1792, 1792], P('ckpt', 'tok'), may hold values from -1 to 2
Outputs:
- consensus: bfloat16 [8192, 1792], P('tok')
- rotation_next: bfloat16 [4, 1792, 1792], P('ckpt', 'tok')
Inputs may be any that keep to these rules, and one draw needn't show every extreme that they name: Each row of a shard of 128 rows appears once in that shard's pairing.
All inputs are finite; a program needn't handle non-finite values.
Results may differ from a plain program's by a relative error of at most 0.011.
Values may be sent and summed in bfloat16 or wider, within the bound.
A program may use at most 64 MiB of HBM per device.

v0:
```python
import math

import jax
import jax.numpy as jnp
from jax import lax
from jax.sharding import PartitionSpec as P


def apply_once(vector, whole):
    inner = lax.dot_general(
        vector.astype(jnp.bfloat16),
        whole,
        (((1,), (1,)), ((), ())),
        preferred_element_type=jnp.float32,
    ).astype(jnp.bfloat16)
    return jnp.dot(inner, whole, preferred_element_type=jnp.float32)


def normalize(own_cov, feature_width):
    squares = lax.psum(jnp.sum(own_cov * own_cov), "tok")
    return (own_cov / (2.0 * jnp.sqrt(squares / feature_width + 1e-06))).astype(jnp.bfloat16)


def block_form(aligned, consensus, devices, column_groups, send_fn, collect_fn):
    row_count, feature_width = aligned.shape
    row_groups = devices // column_groups
    row_width = feature_width // row_groups
    col_width = feature_width // column_groups
    aligned_cols = jnp.repeat(
        aligned.reshape(row_count, row_groups, row_width).transpose(1, 0, 2), column_groups, axis=0
    ).reshape(devices * row_count, row_width)
    consensus_cols = jnp.tile(
        consensus.reshape(row_count, column_groups, col_width).transpose(1, 0, 2),
        (row_groups, 1, 1),
    ).reshape(devices * row_count, col_width)
    aligned_all, consensus_all = send_fn(aligned_cols, consensus_cols)
    own_cov = lax.dot_general(
        aligned_all, consensus_all, (((0,), (0,)), ((), ())), preferred_element_type=jnp.float32
    )
    start_block = normalize(own_cov, feature_width)
    pieces = collect_fn(start_block)
    return (
        pieces.reshape(row_groups, column_groups, row_width, col_width)
        .transpose(0, 2, 1, 3)
        .reshape(feature_width, feature_width)
    )


def shards(features, pairing, rotation):
    own_rows = features[0]
    own_order = pairing[0, 0]
    rot_rows = rotation[0]
    feature_width = own_rows.shape[1]
    aligned = jnp.take(own_rows, own_order, axis=0)
    rotated = jnp.dot(
        aligned,
        lax.all_gather(rot_rows, "tok", axis=0, tiled=True),
        preferred_element_type=jnp.float32,
    ).astype(jnp.bfloat16)
    summed = lax.psum(rotated.astype(jnp.float32).astype(jnp.bfloat16), "ckpt").astype(jnp.float32)
    consensus = (summed / lax.axis_size("ckpt")).astype(jnp.bfloat16)
    devices = lax.axis_size("tok")
    slab_rows = feature_width // devices

    def send_narrow(left, right):
        return (
            lax.all_to_all(left, "tok", split_axis=0, concat_axis=0, tiled=True),
            lax.all_to_all(right, "tok", split_axis=0, concat_axis=0, tiled=True),
        )

    def collect_narrow(block):
        return lax.all_gather(block, "tok", axis=0, tiled=True)

    whole = block_form(aligned, consensus, devices, min(devices, 8), send_narrow, collect_narrow)
    start_rows = lax.dynamic_slice_in_dim(whole, lax.axis_index("tok") * slab_rows, slab_rows, 0)
    first = 1.5 * start_rows.astype(jnp.float32) - 0.5 * apply_once(start_rows, whole)
    upper = 1.5 * first - 0.5 * apply_once(first, whole)
    middle = apply_once(upper, whole)
    cubic = 1.5 * middle - 0.5 * apply_once(middle, whole)
    rotation_next = (math.sqrt(feature_width) * (1.5 * first - 0.5 * cubic)).astype(jnp.bfloat16)
    return (consensus, rotation_next[None])


def solution(mesh):
    placed = (P("ckpt", "tok", None), P("ckpt", "tok", None), P("ckpt", "tok", None))
    return jax.shard_map(
        shards,
        mesh=mesh,
        in_specs=placed,
        out_specs=(P("tok", None), P("ckpt", "tok", None)),
        check_vma=False,
    )
```

profile of v0, /device:TPU:1, one launch (start us, length us, event | category | flops | bytes accessed | tf_op | source)
XLA Modules:
  0.0 733.9 jit_solution(13692629428495231626)
XLA Ops:
  7.2 0.0 copy-start
  7.2 0.0 all-gather.6.cloned.1.call-start
  7.2 1.8 copy.15
  9.0 0.0 all-gather.6.cloned.1.call-update
  9.0 0.7 fusion.25
  9.7 0.0 copy-done
  9.7 0.9 gather_fusion
  10.6 0.3 copy.16
  10.9 0.7 compare_and_fusion
  11.6 2.4 broadcast_in_dim.24
  14.0 15.8 %all-to-all-start = ((bf16[64,128,224]{1,2,0:T(8,128)(2,1)}), bf16[64,128,224]{1,2,0:T(8,128)(2,1)}, u32[]{:S(2)}, u32[]{:S(2)}) async-start(bf16[64,128,224]{1,2,0:T(8,128)(2,1)} %bitcast.41), calls=%async_computation | async-start | bytes 7340032 | tf_op jit(solution)/shard_map/all_to_all | solution.py:67
  29.7 0.0 all-reduce.2.cloned.1.call-start
  29.8 180.5 %all-gather.6.cloned.1.call-done = bf16[1,1792,1792]{2,0,1:T(2,128)(2,1)} async-done(((bf16[1,28,1792]{2,0,1:T(2,128)(2,1)}), bf16[1,1792,1792]{2,0,1:T(2,128)(2,1)}) %all-gather.6.cloned.1.call-update) | async-done | bytes 6422544 | tf_op jit(solution)/shard_map/all_gather | solution.py:57
  210.3 6.5 fusion.3
  216.8 0.0 all-reduce.2.cloned.1.call-update
  216.8 0.0 all-gather.4.cloned.1.call-start
  216.9 43.3 %all-reduce.2.cloned.1.call-done = bf16[128,1792]{1,0:T(8,128)(2,1)} async-done(((bf16[128,1792]{1,0:T(8,128)(2,1)}), bf16[128,1792]{1,0:T(8,128)(2,1)}) %all-reduce.2.cloned.1.call-update) | async-done | bytes 458768 | tf_op jit(solution)/shard_map/psum | solution.py:60
  260.2 1.1 multiply_convert_fusion
  261.3 0.0 copy-start.1
  261.3 0.3 copy.17
  261.5 0.0 all-to-all-done
  261.6 0.6 tile.8
  262.2 96.3 %all_to_all.15 = bf16[64,128,224]{1,2,0:T(8,128)(2,1)S(1)} all-to-all(bf16[64,128,224]{1,2,0:T(8,128)(2,1)S(1)} %bitcast.42), channel_id=1, replica_groups=mesh['ckpt'=4,'tok'=64] {'tok'}, dimensions={0} | all-to-all | bytes 7340032 | tf_op jit(solution)/shard_map/all_to_all | solution.py:68
  358.5 3.8 multiply_reduce_fusion
  362.2 0.0 copy-done.1
  362.2 191.2 %psum.15 = f32[]{:T(128)} all-reduce(f32[]{:T(128)} %get-tuple-element.2), channel_id=1, replica_groups=mesh['ckpt'=4,'tok'=64] {'tok'}, use_global_device_ids=true, to_apply=%region_2.3 | all-reduce | flops 1 | bytes 8 | tf_op jit(solution)/shard_map/psum | solution.py:20
  554.2 0.7 divide_convert_fusion
  554.8 0.0 all-gather.4.cloned.1.call-update
  554.9 117.2 %all-gather.4.cloned.1.call-done = bf16[14336,224]{1,0:T(8,128)(2,1)} async-done(((bf16[224,224]{1,0:T(8,128)(2,1)}), bf16[14336,224]{1,0:T(8,128)(2,1)}) %all-gather.4.cloned.1.call-update) | async-done | bytes 6422544 | tf_op jit(solution)/shard_map/all_gather | solution.py:72
  672.0 10.5 %copy.18 = bf16[8,224,8,224]{3,2,1,0:T(8,128)(2,1)} copy(bf16[8,224,8,224]{3,1,2,0:T(8,128)(2,1)} %bitcast.43) | data formatting | bytes 12845056 | tf_op jit(solution)/shard_map/transpose | solution.py:44
  682.6 13.7 %reshape.66 = bf16[1792,1792]{1,0:T(8,128)(2,1)} reshape(bf16[8,224,8,224]{3,2,1,0:T(8,128)(2,1)} %copy.18) | data formatting | bytes 12845056 | tf_op jit(solution)/shard_map/reshape | solution.py:45
  696.3 7.7 %fusion.10 = f32[28,1792]{1,0:T(8,128)S(1)} fusion(bf16[1792,1792]{1,0:T(8,128)(2,1)} %reshape.66, s32[]{:T(128)S(6)} %select_n.30), kind=kOutput, calls=%fused_computation.12 | convolution fusion | flops 359912448 | bytes 13276160 | tf_op jit(solution)/shard_map/dot_general | solution.py:16
  704.0 7.6 %fusion.12 = bf16[28,1792]{1,0:T(8,128)(2,1)S(1)} fusion(bf16[1792,1792]{1,0:T(8,128)(2,1)} %reshape.66, f32[28,1792]{1,0:T(8,128)S(1)} %fusion.10), kind=kOutput, calls=%fused_computation.14 | convolution fusion | flops 359962624 | bytes 6723584 | tf_op jit(solution)/shard_map/dot_general | solution.py:16
  711.6 7.6 %fusion.15 = f32[28,1792]{1,0:T(8,128)S(1)} fusion(bf16[1792,1792]{1,0:T(8,128)(2,1)} %reshape.66, bf16[28,1792]{1,0:T(8,128)(2,1)S(1)} %fusion.12), kind=kOutput, calls=%fused_computation.22 | convolution fusion | flops 359711744 | bytes 6723584 | tf_op jit(solution)/shard_map/dot_general | solution.py:16
  719.1 8.2 %fusion.14 = bf16[1,28,1792]{2,1,0:T(8,128)(2,1)} fusion(bf16[1792,1792]{1,0:T(8,128)(2,1)} %reshape.66, f32[28,1792]{1,0:T(8,128)S(1)} %fusion.15, f32[28,1792]{1,0:T(8,128)S(1)} %fusion.10), kind=kOutput, calls=%fused_computation.20 | convolution fusion | flops 360163328 | bytes 6924288 | tf_op jit(solution)/shard_map/dot_general | solution.py:16
  (2 shorter events, 0.1 us)
Async XLA Ops:
  7.2 2.5 copy-start
  7.2 203.1 %all-gather.6.cloned.1.call-start = ((), (), s32[]{:S(2)}) async-start(), calls=%async_computation.4 | async-start | bytes 13045760 | tf_op jit(solution)/shard_map/all_gather | solution.py:57
  14.0 247.6 %all-to-all-start = ((bf16[64,128,224]{1,2,0:T(8,128)(2,1)}), bf16[64,128,224]{1,2,0:T(8,128)(2,1)}, u32[]{:S(2)}, u32[]{:S(2)}) async-start(bf16[64,128,224]{1,2,0:T(8,128)(2,1)} %bitcast.41), calls=%async_computation | async-start | bytes 7340032 | tf_op jit(solution)/shard_map/all_to_all | solution.py:67
  29.7 230.4 %all-reduce.2.cloned.1.call-start = ((), (), s32[]{:S(2)}) async-start(), calls=%async_computation.2 | async-start | bytes 917504 | tf_op jit(solution)/shard_map/psum | solution.py:60
  216.8 455.2 %all-gather.4.cloned.1.call-start = ((), (), s32[]{:S(2)}) async-start(), calls=%async_computation.3 | async-start | bytes 7454720 | tf_op jit(solution)/shard_map/all_gather | solution.py:72
  261.3 101.0 %copy-start.1 = (bf16[128,1792]{1,0:T(8,128)(2,1)}, bf16[128,1792]{1,0:T(8,128)(2,1)S(1)}, u32[]{:S(2)}) copy-start(bf16[128,1792]{1,0:T(8,128)(2,1)S(1)} %multiply_convert_fusion) | copy-start | bytes 1376260
Sparse Core Ops, SparseCore 0:
  12.2 198.0 all-gather.5
  216.9 43.1 all-reduce.1
  555.0 117.0 all-gather.3
where the time goes:
time: 735 us; the launch traced here: 734 us
  waiting for transfers between devices  341 us (46%)
  blocking collectives  288 us (39%)
  matrix products  41.3 us (6%)
  local copies, waits for them, and re-layouts  30.5 us (4%)
  starting transfers between devices  15.9 us (2%)
  between operations  14.5 us (2%)
    psum x1, blocking collectives, normalize(): squares = lax.psum(jnp.sum(own_cov * own_cov), 'tok')  191 us
    all_gather x1, waiting for transfers between devices, shards(): lax.all_gather(rot_rows, 'tok', axis=0, tiled=True)  181 us
    all_gather x1, waiting for transfers between devices, collect_narrow(): return lax.all_gather(block, 'tok', axis=0, tiled=True)  117 us
    all_to_all x1, blocking collectives, send_narrow(): lax.all_to_all(right, 'tok', split_axis=0, concat_axis=0, tiled=True)  96.3 us
    psum x1, waiting for transfers between devices, shards(): lax.psum(rotated.astype(jnp.float32).astype(jnp.bfloat16), 'ckpt')  43.3 us
    dot_general x4, matrix products, apply_once(): return jnp.dot(inner, whole, preferred_element_type=jnp.float32)  31.1 us
    all_to_all x1, starting transfers between devices, send_narrow(): lax.all_to_all(left, 'tok', split_axis=0, concat_axis=0, tiled=True)  15.8 us
  transfers between devices with their start and end apart: 4, of which 3 were waited for; matrix products, arithmetic and copies ran while one was open for 2% of the time, Pallas kernels for 0%

commit v1 on v0

v1 whole, which is shorter than its diff:
```python
import functools
import math

import jax
import jax.numpy as jnp
from jax import lax
from jax.experimental import pallas as pl
from jax.experimental.pallas import tpu as pltpu
from jax.sharding import PartitionSpec as P

MESH = pl.DeviceIdType.MESH
BF16, F32 = jnp.bfloat16, jnp.float32
W = 1792
H = W // 2
ROWS = 28
PAD = 32
T = 128
BLK = 112
N_SEM = 128


def dot(left, right):
    return jnp.dot(left, right, preferred_element_type=F32)


def dot_nt(left, right):
    return lax.dot_general(left, right, (((1,), (1,)), ((), ())), preferred_element_type=F32)


def m4(value):
    return lax.rem(value + 8, 4)


def kernel(
    feat, pair, rot, cons_out, next_out,
    rbuf, rsend, apad, at, racc, rotq, rotr, cons, crx,
    tx1, rx1, tx2, rx2, acc, tx3, rx3, tx4, rx4, txz, rxz, sbuf,
    ptx, prx, qtx, qrx, ofin, orx, ssem, rsem,
):
    ck = lax.axis_index("ckpt")
    tok = lax.axis_index("tok")
    core = lax.rem(tok, 2)
    x = lax.rem(lax.div(tok, 2), 4)
    zh = lax.rem(lax.div(tok, 8), 2)
    y = lax.div(tok, 16)
    a = x + core * (y - x)
    b = y + core * (x - y)

    def xy(i, j):
        return i + core * (j - i), j + core * (i - j)

    def chip(i, j, plane):
        px, py = xy(m4(i), m4(j))
        return (py * 2 + plane) * 4 + px

    def dev(i, j):
        return (ck, chip(i, j, zh) * 2 + core)

    right1, left1, right2, left2 = dev(a + 1, b), dev(a - 1, b), dev(a, b + 1), dev(a, b - 1)
    other = (ck, tok + 1 - 2 * core)
    far = (ck, ((y * 2 + 1 - zh) * 4 + x) * 2 + core)
    members = [m4(ck + d) for d in (1, 2, 3)]

    barrier = pltpu.get_barrier_semaphore()
    partners = [right1, left1, right2, left2, other, far] + [(m, tok) for m in members]
    for device in partners:
        pl.semaphore_signal(barrier, inc=1, device_id=device, device_id_type=MESH)
    pl.semaphore_wait(barrier, len(partners))

    sends = []

    def send(src, dst, device):
        slot = len(sends)
        assert slot < N_SEM
        copy = pltpu.make_async_remote_copy(
            src_ref=src,
            dst_ref=dst,
            send_sem=ssem.at[slot],
            recv_sem=rsem.at[slot],
            device_id=device,
            device_id_type=MESH,
        )
        copy.start()
        sends.append(copy)
        return copy

    def gather(part, meanwhile=None):
        def move(i, j, k, device):
            ref = part(i, j, k)
            return send(ref, ref, device)

        first_r, first_l = move(a, b, None, right1), move(a, b, None, left1)
        second = {}

        def spread(i):
            second[i] = (move(a + i, b, None, right2), move(a + i, b, None, left2))

        halves = {}

        def relay(i):
            second[i][0].wait_recv()
            low = move(a + i, b - 1, 0, right2)
            second[i][1].wait_recv()
            high = move(a + i, b + 1, 1, left2)
            halves[i] = (low, high)

        spread(0)
        if meanwhile is not None:
            meanwhile()
        first_r.wait_recv()
        half_r = move(a - 1, b, 0, right1)
        spread(-1)
        first_l.wait_recv()
        half_l = move(a + 1, b, 1, left1)
        spread(1)
        relay(0)
        half_r.wait_recv()
        half_l.wait_recv()
        spread(2)
        for i in (-1, 1, 2):
            relay(i)
        for i in (0, -1, 1, 2):
            halves[i][0].wait_recv()
            halves[i][1].wait_recv()

    def halfcols(value, index):
        return jnp.where(index == 0, value[:, :H], value[:, H:])

    own_rot = rot[0].astype(F32)
    zeros = jnp.zeros((PAD - ROWS, H), BF16)
    rbuf[tok, 0:ROWS, :] = halfcols(own_rot, core).astype(BF16)
    rbuf[tok, ROWS:PAD, :] = zeros
    rsend[0:ROWS, :] = halfcols(own_rot, 1 - core).astype(BF16)
    rsend[ROWS:PAD, :] = zeros
    swap = send(rsend, rbuf.at[tok], other)

    def rot_part(plane):
        def part(i, j, k):
            base = chip(i, j, plane) * 2
            return rbuf.at[pl.ds(base, 2)] if k is None else rbuf.at[base + k]

        return part

    def align():
        order = pair[0]
        hot_t = lax.broadcasted_iota(jnp.int32, (T, T), 0) == jnp.broadcast_to(order, (T, T))
        hot = jnp.transpose(jnp.where(hot_t, 1.0, 0.0)).astype(BF16)
        for n in range(7):
            cols = dot(hot, feat[0, :, 256 * n : 256 * n + 256])
            at[core, 16 * n : 16 * n + 16] = jnp.transpose(cols).astype(BF16).reshape(16, 16, T)
        for g in range(8):
            start = (224 * g) // 128 * 128
            width = min(384, W - start)
            src = lax.broadcasted_iota(jnp.int32, (width, 256), 0)
            dst = lax.broadcasted_iota(jnp.int32, (width, 256), 1)
            row = dst & 31
            want = (224 * g - start) + (dst >> 5) * ROWS + row
            place = jnp.where((src == want) & (row < ROWS), 1.0, 0.0).astype(BF16)
            window = dot(hot, feat[0, :, start : start + width]).astype(BF16)
            apad[core, g] = dot(window, place).astype(BF16)

    swap.wait_recv()
    own_chunk = rot_part(zh)(a, b, None)
    far_chunk = send(own_chunk, own_chunk, far)
    gather(rot_part(zh), align)
    aligned = [send(apad.at[core], apad.at[core], other), send(at.at[core], at.at[core], other)]
    far_chunk.wait_recv()
    gather(rot_part(1 - zh))
    for copy in aligned:
        copy.wait_recv()

    racc[...] = jnp.zeros_like(racc)

    def rotate(g, carry):
        left = jnp.concatenate([apad[0, g], apad[1, g]], axis=0)
        racc[...] += dot(left, rbuf[pl.ds(8 * g, 8)].reshape(8 * PAD, H))
        return carry

    lax.fori_loop(0, 8, rotate, 0)
    rotq[...] = racc[...].astype(BF16).reshape(4, 64, H)

    quarters = [send(rotq.at[m], rotr.at[ck], (m, tok)) for m in members]
    total = rotq[ck].astype(F32)
    for d, copy in zip((3, 2, 1), quarters):
        copy.wait_recv()
        total += rotr[m4(ck + d)].astype(F32)
    cons[ck] = (total * 0.25).astype(BF16)
    quarters = [send(cons.at[ck], cons.at[ck], (m, tok)) for m in members]
    for copy in quarters:
        copy.wait_recv()
    back = send(cons.at[pl.ds(2 * (1 - core), 2)], crx, other)

    cvalue = cons[...].reshape(2 * T, H)

    def block(i, j):
        px, py = xy(m4(i), m4(j))
        return (py * 4 + px) * 7

    def local(i, j):
        n = block(i, j)
        left = jnp.concatenate(
            [at[0, pl.ds(n, 7)].reshape(BLK, T), at[1, pl.ds(n, 7)].reshape(BLK, T)], axis=1
        )
        return dot(left, cvalue)

    def tiles(value):
        return value.astype(BF16).reshape(-1, 16, H)

    def wide(value):
        return value.astype(F32).reshape(-1, H)

    order = (2, 1, -1, 0)
    step1 = []
    for n, j in enumerate(order):
        tx1[n] = tiles(local(a + 2, b + j))
        step1.append(
            (
                send(tx1.at[n, 0:4], rx1.at[n, 0:4], right1),
                send(tx1.at[n, 4:7], rx1.at[n, 4:7], left1),
            )
        )
    step2 = []
    for n, j in enumerate(order):
        acc[...] = local(a + 1, b + j)
        step1[n][0].wait_recv()
        acc[0:64] += wide(rx1[n, 0:4])
        tx2[0, n] = tiles(acc[...])
        to_right = send(tx2.at[0, n], rx2.at[0, n], right1)
        acc[...] = local(a - 1, b + j)
        step1[n][1].wait_recv()
        acc[64:112] += wide(rx1[n, 4:7])
        tx2[1, n] = tiles(acc[...])
        step2.append((to_right, send(tx2.at[1, n], rx2.at[1, n], left1)))

    def along(n):
        value = local(a, b + order[n])
        step2[n][0].wait_recv()
        step2[n][1].wait_recv()
        return value + wide(rx2[0, n]) + wide(rx2[1, n])

    tx3[...] = tiles(along(0))
    step3 = (send(tx3.at[0:4], rx3.at[0:4], right2), send(tx3.at[4:7], rx3.at[4:7], left2))
    acc[...] = along(1)
    step3[0].wait_recv()
    acc[0:64] += wide(rx3[0:4])
    tx4[0] = tiles(acc[...])
    to_right = send(tx4.at[0], rx4.at[0], right2)
    acc[...] = along(2)
    step3[1].wait_recv()
    acc[64:112] += wide(rx3[4:7])
    tx4[1] = tiles(acc[...])
    to_left = send(tx4.at[1], rx4.at[1], left2)
    acc[...] = along(3)
    to_right.wait_recv()
    to_left.wait_recv()
    acc[...] += wide(rx4[0]) + wide(rx4[1])
    txz[...] = tiles(acc[...])
    across = send(txz, rxz, far)
    back.wait_recv()

    @pl.when(core == 0)
    def _():
        cons_out[:, :H] = cons[0:2].reshape(T, H)
        cons_out[:, H:] = crx[...].reshape(T, H)

    @pl.when(core == 1)
    def _():
        cons_out[:, H:] = cons[2:4].reshape(T, H)
        cons_out[:, :H] = crx[...].reshape(T, H)

    across.wait_recv()
    own_block = block(a, b)
    sbuf[pl.ds(own_block, 7)] = tiles(acc[...] + wide(rxz[...]))

    def cov_part(i, j, k):
        n = block(i, j)
        if k is None:
            return sbuf.at[pl.ds(n, 7)]
        return sbuf.at[pl.ds(n, 4)] if k == 0 else sbuf.at[pl.ds(n + 4, 3)]

    gather(cov_part)

    def rows(n):
        return sbuf[16 * n : 16 * n + 16].reshape(256, H)

    square = jnp.zeros((1, H), F32)
    for n in range(7):
        value = rows(n).astype(F32)
        square += jnp.sum(value * value, axis=0, keepdims=True)
    qtx[...] = jnp.broadcast_to(jnp.sum(square, axis=1, keepdims=True), (8, 128))
    squares = send(qtx, qrx, other)

    px, py = x, y
    base = (py * 4 + zh * 2 + lax.div(px, 2)) * 7
    dst = lax.broadcasted_iota(jnp.int32, (2 * PAD, BLK), 0)
    src = lax.broadcasted_iota(jnp.int32, (2 * PAD, BLK), 1)
    row = dst & 31
    want = 56 * lax.rem(px, 2) + (dst >> 5) * ROWS + row
    pick = jnp.where((src == want) & (row < ROWS), 1.0, 0.0).astype(BF16)
    raw = dot(pick, sbuf[pl.ds(base, 7)].reshape(BLK, H))

    def apply(vector, n):
        low = vector.astype(BF16)
        for k in range(7):
            ptx[n, :, 256 * k : 256 * k + 256] = dot_nt(low, rows(k))
        copy = send(ptx.at[n], prx.at[n], other)
        copy.wait_recv()
        inner = (ptx[n] + prx[n]).astype(BF16)
        result = dot(inner[:, 0:256], rows(0))
        for k in range(1, 7):
            result += dot(inner[:, 256 * k : 256 * k + 256], rows(k))
        return result

    once = apply(raw, 0)
    squares.wait_recv()
    scale = 2.0 * jnp.sqrt((qtx[0:1, 0:1] + qrx[0:1, 0:1]) / W + 1e-06)
    inverse = 1.0 / scale
    square_inverse = inverse * inverse
    first = (1.5 * raw - 0.5 * (once * square_inverse)) * inverse
    upper = 1.5 * first - 0.5 * (apply(first, 1) * square_inverse)
    middle = apply(upper, 2) * square_inverse
    cubic = 1.5 * middle - 0.5 * (apply(middle, 3) * square_inverse)
    ofin[...] = (math.sqrt(W) * (1.5 * first - 0.5 * cubic)).astype(BF16).reshape(2, PAD, H)
    final = send(ofin.at[1 - core], orx, other)
    final.wait_recv()

    @pl.when(core == 0)
    def _():
        next_out[0, :, :H] = ofin[0, 0:ROWS]
        next_out[0, :, H:] = orx[0:ROWS]

    @pl.when(core == 1)
    def _():
        next_out[0, :, H:] = ofin[1, 0:ROWS]
        next_out[0, :, :H] = orx[0:ROWS]

    for copy in sends:
        copy.wait_send()


def shards(features, pairing, rotation):
    vmem = pl.BlockSpec(memory_space=pltpu.VMEM)
    return pl.pallas_call(
        kernel,
        out_shape=(
            jax.ShapeDtypeStruct((T, W), BF16),
            jax.ShapeDtypeStruct((1, ROWS, W), BF16),
        ),
        in_specs=[vmem] * 3,
        out_specs=(vmem, vmem),
        scratch_shapes=[
            pltpu.VMEM((64, PAD, H), BF16),
            pltpu.VMEM((PAD, H), BF16),
            pltpu.VMEM((2, 8, T, 256), BF16),
            pltpu.VMEM((2, 112, 16, T), BF16),
            pltpu.VMEM((2 * T, H), F32),
            pltpu.VMEM((4, 64, H), BF16),
            pltpu.VMEM((4, 64, H), BF16),
            pltpu.VMEM((4, 64, H), BF16),
            pltpu.VMEM((2, 64, H), BF16),
            pltpu.VMEM((4, 7, 16, H), BF16),
            pltpu.VMEM((4, 7, 16, H), BF16),
            pltpu.VMEM((2, 4, 7, 16, H), BF16),
            pltpu.VMEM((2, 4, 7, 16, H), BF16),
            pltpu.VMEM((BLK, H), F32),
            pltpu.VMEM((7, 16, H), BF16),
            pltpu.VMEM((7, 16, H), BF16),
            pltpu.VMEM((2, 7, 16, H), BF16),
            pltpu.VMEM((2, 7, 16, H), BF16),
            pltpu.VMEM((7, 16, H), BF16),
            pltpu.VMEM((7, 16, H), BF16),
            pltpu.VMEM((112, 16, H), BF16),
            pltpu.VMEM((4, 2 * PAD, W), F32),
            pltpu.VMEM((4, 2 * PAD, W), F32),
            pltpu.VMEM((8, 128), F32),
            pltpu.VMEM((8, 128), F32),
            pltpu.VMEM((2, PAD, H), BF16),
            pltpu.VMEM((PAD, H), BF16),
            pltpu.SemaphoreType.DMA((N_SEM,)),
            pltpu.SemaphoreType.DMA((N_SEM,)),
        ],
        compiler_params=pltpu.CompilerParams(
            collective_id=0, has_side_effects=True, vmem_limit_bytes=60 * 1024 * 1024
        ),
    )(features, pairing, rotation)


def solution(mesh):
    placed = (P("ckpt", "tok", None), P("ckpt", "tok", None), P("ckpt", "tok", None))
    return jax.shard_map(
        shards,
        mesh=mesh,
        in_specs=placed,
        out_specs=(P("tok", None), P("ckpt", "tok", None)),
        check_vma=False,
    )
```

time: 735 us -> 142 us (0.19)
  waiting for transfers between devices: 341 us -> 0 us
  blocking collectives: 288 us -> 0 us
  Pallas kernels: 0 us -> 137 us
  matrix products: 41.3 us -> 0 us
  local copies, waits for them, and re-layouts: 30.5 us -> 2.5 us
  starting transfers between devices: 15.9 us -> 0 us
  between operations: 14.5 us -> 0.65 us
    all_gather x2 -> x0, waiting for transfers between devices: 298 us -> none  [the longest x1 181 us: shards(): lax.all_gather(rot_rows, 'tok', axis=0, tiled=True)]
    psum x1 -> x0, blocking collectives: 191 us -> none  [normalize(): squares = lax.psum(jnp.sum(own_cov * own_cov), 'tok')]
    pallas_call x0 -> x1, Pallas kernels: none -> 137 us  [shards(): pl.pallas_call(kernel, out_shape=(jax.ShapeDtypeStruct((T, W), BF16), jax...]
    all_to_all x1 -> x0, blocking collectives: 96.3 us -> none  [send_narrow(): lax.all_to_all(right, 'tok', split_axis=0, concat_axis=0, tiled=True)]
    psum x1 -> x0, waiting for transfers between devices: 43.3 us -> none  [shards(): lax.psum(rotated.astype(jnp.float32).astype(jnp.bfloat16), 'ckpt')]
    dot_general x6 -> x0, matrix products: 41.3 us -> none  [the longest x4 31.1 us: apply_once(): return jnp.dot(inner, whole, preferred_element_type=jnp.float32)]
    all_to_all x1 -> x0, starting transfers between devices: 15.8 us -> none  [send_narrow(): lax.all_to_all(left, 'tok', split_axis=0, concat_axis=0, tiled=True)]
    reshape x1 -> x0, local copies, waits for them, and re-layouts: 13.7 us -> none  [block_form(): return pieces.reshape(row_groups, column_groups, row_width, col_width).tr...]
  transfers between devices with their start and end apart: 4 -> 0, of which waited for: 3 -> 0; matrix products, arithmetic and copies ran while one was open for 2% -> 0% of each run, Pallas kernels for 0% -> 0%
where the time goes in v1:
time: 142 us; the launch traced here: 140 us
  Pallas kernels  137 us (96%)
  local copies, waits for them, and re-layouts  2.5 us (2%)
    pallas_call x1, Pallas kernels, shards(): pl.pallas_call(kernel, out_shape=(jax.ShapeDtypeStruct((T, W), BF16), jax...  137 us

profile of v1, /device:TPU:1, one launch (start us, length us, event | category | flops | bytes accessed | tf_op | source)
XLA Modules:
  0.0 140.1 jit_solution(17520551782302731827)
XLA Ops:
  0.6 136.9 %shard_map.50 = (bf16[128,1792]{1,0:T(8,128)(2,1)}, bf16[1,28,1792]{2,1,0:T(8,128)(2,1)}) custom-call(bf16[1,128,1792]{2,1,0:T(8,128)(2,1)} %feat.1, s32[1,1,128]{2,1,0:T(1,128)} %pair.1, bf16[1,28,1792]{2,1,0:T(8,128)(2,1)} %rot.1), custom_call_target="tpu_custom_call" | custom-call | tf_op jit(solution)/shard_map/pallas_call | solution.py:343
  137.6 0.0 copy-start
  137.6 1.9 %copy.7 = bf16[128,1792]{1,0:T(8,128)(2,1)} copy(bf16[128,1792]{1,0:T(8,128)(2,1)} %get-tuple-element.4) | data formatting | bytes 917504
  139.4 0.0 copy-done
  139.4 0.6 copy.8
Async XLA Ops:
  137.6 1.9 %copy-start = (bf16[1,28,1792]{2,1,0:T(8,128)(2,1)S(1)}, bf16[1,28,1792]{2,1,0:T(8,128)(2,1)}, u32[]{:S(2)}) copy-start(bf16[1,28,1792]{2,1,0:T(8,128)(2,1)} %get-tuple-element.5) | copy-start | bytes 301060

commit v2 on v0

v2 whole, which is shorter than its diff:
```python
import heapq
import math

import jax
import jax.numpy as jnp
from jax import lax
from jax.experimental import pallas as pl
from jax.experimental.pallas import tpu as pltpu
from jax.sharding import PartitionSpec as P

MESH = pl.DeviceIdType.MESH
BF16, F32 = jnp.bfloat16, jnp.float32
W = 1792
H = W // 2
ROWS = 28
PAD = 32
T = 128
BLK = 112
WIDTHS = (256, 256, 256, 128)
STARTS = tuple(sum(WIDTHS[:p]) for p in range(len(WIDTHS)))
PARTS = range(len(WIDTHS))
N_SEND, N_RECV = 48, 220
NEAR1 = (0, 1, 2, 3)
GFAST = (0,)
FAST = (3,)

RATE, CHIP_RATE = 90e3, 600e3
HOP, CHIP_HOP, FURTHER = 2.4, 1.6, 0.7
BACKLOG = 0.3
GROUPS = {1: 2, 3: 2, 5: 2, 6: 1}


def scratch():
    out = []
    for p, w in enumerate(WIDTHS):
        for name, shape, dtype in (
            ("rbuf", (64, PAD, w), BF16),
            ("rsend", (PAD, w), BF16),
            ("rotq", (4, 64, w), BF16),
            ("rotr", (4, 64, w), BF16),
            ("cons", (4, 64, w), BF16),
            ("crx", (2, 64, w), BF16),
            ("tx1", (4, 7, 16, w), BF16),
            ("rx1", (4, 7, 16, w), BF16),
            ("tx2", (2, 4, 7, 16, w), BF16),
            ("rx2", (2, 4, 7, 16, w), BF16),
            ("acc", (3, 4, BLK, w), F32),
            ("tx3", (7, 16, w), BF16),
            ("rx3", (7, 16, w), BF16),
            ("tx4", (2, 7, 16, w), BF16),
            ("rx4", (2, 7, 16, w), BF16),
            ("txz", (7, 16, w), BF16),
            ("rxz", (7, 16, w), BF16),
            ("sbuf", (112, 16, w), BF16),
            ("ofin", (2, PAD, w), BF16),
            ("orx", (PAD, w), BF16),
            ("racc", (2 * T, w), F32),
        ):
            out.append(((name, p), pltpu.VMEM(shape, dtype)))
    out += [
        (("aown", None), pltpu.VMEM((T, W), BF16)),
        (("apad", None), pltpu.VMEM((2, 8, T, 256), BF16)),
        (("at", None), pltpu.VMEM((2, 112, 16, T), BF16)),
        (("ptx", None), pltpu.VMEM((4, 7, 2 * PAD, 256), F32)),
        (("prx", None), pltpu.VMEM((4, 7, 2 * PAD, 256), F32)),
        (("qtx", None), pltpu.VMEM((8, 128), F32)),
        (("qrx", None), pltpu.VMEM((8, 128), F32)),
        (("ssem", None), pltpu.SemaphoreType.DMA((N_SEND,))),
        (("rsem", None), pltpu.SemaphoreType.DMA((N_RECV,))),
    ]
    return out


def dot(left, right):
    return jnp.dot(left, right, preferred_element_type=F32)


def dot_nt(left, right):
    return lax.dot_general(left, right, (((1,), (1,)), ((), ())), preferred_element_type=F32)


def m4(value):
    return lax.rem(value + 8, 4)


class Timeline:
    def __init__(self, ssem, rsem):
        self.ssem, self.rsem = ssem, rsem
        self.now, self.free, self.queue, self.idle, self.sends = 0.0, {}, [], [], []
        self.pushed = self.slots = 0

    def cost(self, us):
        self.now += us

    def slot(self):
        self.slots += 1
        assert self.slots <= N_RECV
        return self.slots - 1

    def send(self, src, dst, device, lane, slot=None):
        turn = len(self.sends)
        if turn >= N_SEND:
            self.sends[turn - N_SEND].wait_send()
        copy = pltpu.make_async_remote_copy(
            src_ref=src,
            dst_ref=dst,
            send_sem=self.ssem.at[turn % N_SEND],
            recv_sem=self.rsem.at[self.slot() if slot is None else slot],
            device_id=device,
            device_id_type=MESH,
        )
        copy.start()
        self.sends.append(copy)
        size = math.prod(src.shape) * jnp.dtype(src.dtype).itemsize
        names, rate, latency = {
            "R": ("R", RATE, HOP),
            "L": ("L", RATE, HOP),
            "RL": ("RL", RATE, HOP + FURTHER),
            "core": ("C", CHIP_RATE, CHIP_HOP),
            "z": ("Z", RATE / 2, HOP + FURTHER),
            "far": ("Z", RATE / 4, HOP + 3 * FURTHER),
        }[lane]
        self.now += 0.02
        for name in names:
            self.free[name] = max(self.now, self.free.get(name, 0.0)) + size / rate
        return copy.wait_recv, max(self.free[name] for name in names) + latency

    def together(self, slot, ref, sent):
        return pltpu.make_async_copy(ref, ref, self.rsem.at[slot]).wait, max(arrival for _, arrival in sent)

    def finish(self):
        for copy in self.sends[-N_SEND:]:
            copy.wait_send()

    def after(self, sent, action):
        wait, arrival = sent
        self.pushed += 1
        heapq.heappush(self.queue, (arrival, self.pushed, wait, action))

    def later(self, rank, action):
        self.pushed += 1
        heapq.heappush(self.idle, (rank, self.pushed, action))

    def run(self):
        while self.queue or self.idle:
            if self.idle:
                quiet = max(self.free.get("R", 0.0), self.free.get("L", 0.0)) - BACKLOG
                if not self.queue or quiet <= max(self.now, self.queue[0][0]):
                    self.now = max(self.now, quiet)
                    heapq.heappop(self.idle)[2]()
                    continue
            arrival, _, wait, action = heapq.heappop(self.queue)
            self.now = max(self.now, arrival)
            wait()
            action()


def when_all(count, action):
    left = [count]

    def one():
        left[0] -= 1
        if not left[0]:
            action()

    return one


def nothing():
    pass


def kernel(feat, pair, rot, cons_out, next_out, *refs):
    buf = {name: ref for (name, _), ref in zip(scratch(), refs)}
    aown, apad, at, ptx, prx, qtx, qrx, ssem, rsem = [
        buf[name, None] for name in ("aown", "apad", "at", "ptx", "prx", "qtx", "qrx", "ssem", "rsem")
    ]
    ck = lax.axis_index("ckpt")
    tok = lax.axis_index("tok")
    core = lax.rem(tok, 2)
    x = lax.rem(lax.div(tok, 2), 4)
    zh = lax.rem(lax.div(tok, 8), 2)
    y = lax.div(tok, 16)
    a = x + core * (y - x)
    b = y + core * (x - y)

    def xy(i, j):
        i, j = m4(i), m4(j)
        return i + core * (j - i), j + core * (i - j)

    def chip(i, j, plane):
        px, py = xy(i, j)
        return (py * 2 + plane) * 4 + px

    def dev(i, j):
        return (ck, chip(i, j, zh) * 2 + core)

    right1, left1, right2, left2 = dev(a + 1, b), dev(a - 1, b), dev(a, b + 1), dev(a, b - 1)
    across1, across2 = dev(a + 2, b), dev(a, b + 2)
    other = (ck, tok + 1 - 2 * core)
    far, far_other = [(ck, ((y * 2 + 1 - zh) * 4 + x) * 2 + c) for c in (core, 1 - core)]
    members = [m4(ck + d) for d in (1, 2, 3)]

    barrier = pltpu.get_barrier_semaphore()
    partners = [right1, left1, across1, right2, left2, across2, other, far, far_other] + [(m, tok) for m in members]
    for device in partners:
        pl.semaphore_signal(barrier, inc=1, device_id=device, device_id_type=MESH)
    pl.semaphore_wait(barrier, len(partners))

    line = Timeline(ssem, rsem)
    send, after = line.send, line.after

    def gather(part, done, direct1, direct2):
        late, lates = line.slot(), []

        def move(i, j, k, device, lane, slot=None):
            ref = part(i, j, k)
            return send(ref, ref, device, lane, slot)

        def finish():
            after(line.together(late, part(None, None, 12 if direct2 else 4), lates), done)

        relayed = when_all(8, finish)

        def spread(i):
            if direct2:
                lates.append(move(a + i, b, None, right2, "R", late))
                lates.append(move(a + i, b, None, left2, "L", late))
                lates.append(move(a + i, b, None, across2, "RL", late))
                if len(lates) == 12:
                    finish()
                return

            def half():
                lates.append(move(a + i, b - 1, 0, right2, "R", late))
                relayed()

            def half_back():
                lates.append(move(a + i, b + 1, 1, left2, "L", late))
                relayed()

            after(move(a + i, b, None, right2, "R"), half)
            after(move(a + i, b, None, left2, "L"), half_back)

        def from_across():
            spread(2)

        halves, pair = [], None if direct1 else line.slot()
        both = when_all(2, lambda: after(line.together(pair, part(None, None, 1), halves), from_across))

        def from_left():
            if not direct1:
                halves.append(move(a - 1, b, 0, right1, "R", pair))
                both()
            spread(-1)

        def from_right():
            if not direct1:
                halves.append(move(a + 1, b, 1, left1, "L", pair))
                both()
            spread(1)

        after(move(a, b, None, right1, "R"), from_left)
        after(move(a, b, None, left1, "L"), from_right)
        if direct1:
            after(move(a, b, None, across1, "RL"), from_across)
        spread(0)

    swaps, fars = [], []
    for p, w in enumerate(WIDTHS):
        rbuf, rsend = buf["rbuf", p], buf["rsend", p]
        low = rot[0, :, STARTS[p] : STARTS[p] + w].astype(F32)
        high = rot[0, :, H + STARTS[p] : H + STARTS[p] + w].astype(F32)
        zeros = jnp.zeros((PAD - ROWS, w), BF16)
        rsend[0:ROWS, :] = jnp.where(core == 0, high, low).astype(BF16)
        rsend[ROWS:PAD, :] = zeros
        swaps.append(send(rsend, rbuf.at[tok], other, "core"))
        rbuf[tok, 0:ROWS, :] = jnp.where(core == 0, low, high).astype(BF16)
        rbuf[tok, ROWS:PAD, :] = zeros
        slot = line.slot()
        sent = [
            send(rsend, rbuf.at[tok], far_other, "far", slot),
            send(rbuf.at[tok], rbuf.at[tok], far, "far", slot),
        ]
        fars.append(line.together(slot, rbuf.at[pl.ds(0, 2)], sent))

    def begin(p):
        rbuf = buf["rbuf", p]

        def part(plane):
            def of(i, j, k):
                if i is None:
                    return rbuf.at[pl.ds(0, 2 * k)]
                base = chip(i, j, plane) * 2
                return rbuf.at[pl.ds(base, 2)] if k is None else rbuf.at[base + k]

            return of

        done = when_all(2 if p else 4, lambda: rotate(p))

        def near():
            gather(part(zh), done, p in NEAR1, p in GFAST)
            if p == 0:
                align(done)

        def distant():
            gather(part(1 - zh), done, p in NEAR1, p in GFAST)
            if p + 1 in PARTS:
                begin(p + 1)

        after(swaps[p], lambda: line.later(2 * p, near))
        after(fars[p], lambda: line.later(2 * p + 1, distant))

    def align(done):
        order = pair[0]
        hot_t = lax.broadcasted_iota(jnp.int32, (T, T), 0) == jnp.broadcast_to(order, (T, T))
        hot = jnp.transpose(jnp.where(hot_t, 1.0, 0.0)).astype(BF16)
        for n in range(7):
            aown[:, 256 * n : 256 * n + 256] = dot(hot, feat[0, :, 256 * n : 256 * n + 256]).astype(BF16)
        for g in range(8):
            start = (224 * g) // 128 * 128
            width = min(384, W - start)
            src = lax.broadcasted_iota(jnp.int32, (width, 256), 0)
            dst = lax.broadcasted_iota(jnp.int32, (width, 256), 1)
            row = dst & 31
            want = (224 * g - start) + (dst >> 5) * ROWS + row
            place = jnp.where((src == want) & (row < ROWS), 1.0, 0.0).astype(BF16)
            apad[core, g] = dot(aown[:, start : start + width], place).astype(BF16)
        dst = lax.broadcasted_iota(jnp.int32, (448, 512), 0)
        src = lax.broadcasted_iota(jnp.int32, (448, 512), 1)
        px = sum((dst >= BLK * n).astype(jnp.int32) for n in (1, 2, 3))
        dst = dst - BLK * px
        plane = (dst >= 56).astype(jnp.int32)
        want = 224 * plane + 56 * px + dst - 56 * plane
        places = [jnp.where(src == want + offset, 1.0, 0.0).astype(BF16) for offset in (0, 64)]
        for n in range(4):
            start = 448 * n // 128 * 128
            window = dot_nt(places[n % 2], aown[:, start : start + 512])
            at[core, 28 * n : 28 * n + 28] = window.astype(BF16).reshape(28, 16, T)
        after(send(apad.at[core], apad.at[core], other, "core"), done)
        after(send(at.at[core], at.at[core], other, "core"), done)
        line.cost(3.0)

    def rotate(p):
        w, racc, rbuf, rotq, rotr = WIDTHS[p], buf["racc", p], buf["rbuf", p], buf["rotq", p], buf["rotr", p]
        racc[...] = jnp.zeros_like(racc)

        def step(g, carry):
            left = jnp.concatenate([apad[0, g], apad[1, g]], axis=0)
            racc[...] += dot(left, rbuf[pl.ds(8 * g, 8)].reshape(8 * PAD, w))
            return carry

        lax.fori_loop(0, 8, step, 0)
        rotq[...] = racc[...].astype(BF16).reshape(4, 64, w)
        line.cost(w / 300)
        slot = line.slot()
        sent = [send(rotq.at[m], rotr.at[ck], (m, tok), "z", slot) for m in members]
        after(line.together(slot, rotr.at[pl.ds(0, 3)], sent), lambda: mean(p))

    def mean(p):
        rotq, rotr, cons, crx = buf["rotq", p], buf["rotr", p], buf["cons", p], buf["crx", p]
        total = rotq[ck].astype(F32)
        for m in members:
            total += rotr[m].astype(F32)
        cons[ck] = (total * 0.25).astype(BF16)
        line.cost(0.2)

        def whole():
            after(send(cons.at[pl.ds(2 * (1 - core), 2)], crx, other, "core"), lambda: store(p))
            line.later(10 + p, lambda: reduce_plane(p))

        slot = line.slot()
        sent = [send(cons.at[ck], cons.at[ck], (m, tok), "z", slot) for m in members]
        after(line.together(slot, cons.at[pl.ds(0, 3)], sent), whole)

    def store(p):
        w, cons, crx = WIDTHS[p], buf["cons", p], buf["crx", p]
        low, high = slice(STARTS[p], STARTS[p] + w), slice(H + STARTS[p], H + STARTS[p] + w)

        @pl.when(core == 0)
        def _():
            cons_out[:, low] = cons[0:2].reshape(T, w)
            cons_out[:, high] = crx[...].reshape(T, w)

        @pl.when(core == 1)
        def _():
            cons_out[:, high] = cons[2:4].reshape(T, w)
            cons_out[:, low] = crx[...].reshape(T, w)

        line.cost(0.1)

    def block(i, j):
        px, py = xy(i, j)
        return (py * 4 + px) * 7

    order = (2, 1, -1, 0)

    def reduce_plane(p):
        w = WIDTHS[p]
        tx1, rx1, tx2, rx2, acc = [buf[name, p] for name in ("tx1", "rx1", "tx2", "rx2", "acc")]
        tx3, rx3, tx4, rx4, txz, rxz = [buf[name, p] for name in ("tx3", "rx3", "tx4", "rx4", "txz", "rxz")]
        cvalue = buf["cons", p][...].reshape(2 * T, w)

        def local(i):
            sides = []
            for k in range(2):
                sides.append(
                    jnp.concatenate([at[k, pl.ds(block(i, b + j), 7)].reshape(BLK, T) for j in order], axis=0)
                )
            line.cost(w / 500)
            return dot(jnp.concatenate(sides, axis=1), cvalue).reshape(4, BLK, w)

        def tiles(value):
            return value.astype(BF16).reshape(-1, 16, w)

        def wide(value):
            return value.astype(F32).reshape(-1, w)

        acc[0] = local(a + 2)
        tx1[...] = acc[0].astype(BF16).reshape(4, 7, 16, w)

        def final():
            txz[...] = tiles(acc[2, 3])
            line.cost(0.2)
            after(send(txz, rxz, far, "far"), lambda: spread_cov(p))

        direct2 = p in NEAR1
        slot, sent = line.slot(), []

        def last():
            if len(sent) == (3 if direct2 else 2):
                after(line.together(slot, tx2.at[0, 0 : len(sent)], sent), total)

        def total():
            acc[2, 3] += wide(rx4[0]) + wide(rx4[1])
            if direct2:
                acc[2, 3] += wide(rx3[...])
            line.cost(0.2)
            finals()

        finals = when_all(2, final)
        back = [when_all(1 if direct2 else 2, lambda: go_right()), when_all(1 if direct2 else 2, lambda: go_left())]

        def go_right():
            if not direct2:
                acc[2, 1, 0:64] += wide(rx3[0:4])
            tx4[0] = tiles(acc[2, 1])
            line.cost(0.1)
            sent.append(send(tx4.at[0], rx4.at[0], right2, "R", slot))
            last()

        def go_left():
            if not direct2:
                acc[2, 2, 64:112] += wide(rx3[4:7])
            tx4[1] = tiles(acc[2, 2])
            line.cost(0.1)
            sent.append(send(tx4.at[1], rx4.at[1], left2, "L", slot))
            last()

        def go_across():
            tx3[...] = tiles(acc[2, 0])
            if direct2:
                sent.append(send(tx3, rx3, across2, "RL", slot))
                last()
                return
            after(send(tx3.at[0:4], rx3.at[0:4], right2, "R"), back[0])
            after(send(tx3.at[4:7], rx3.at[4:7], left2, "L"), back[1])

        then = (go_across, back[0], back[1], finals)

        if p in FAST:
            slots = [line.slot() for _ in range(4)]
            sents = [[send(tx1.at[n], rx1.at[n], across1, "RL", slots[n])] for n in range(4)]
            for side, (device, lane) in enumerate(((right1, "R"), (left1, "L"))):
                acc[side] = local(a + 1 - 2 * side)
                tx2[side] = acc[side].astype(BF16).reshape(4, 7, 16, w)
                for n in range(4):
                    sents[n].append(send(tx2.at[side, n], rx2.at[side, n], device, lane, slots[n]))
            acc[2] = local(a)

            def column(n):
                def add():
                    acc[2, n] += wide(rx1[n]) + wide(rx2[0, n]) + wide(rx2[1, n])
                    line.cost(0.2)
                    then[n]()

                after(line.together(slots[n], tx1.at[0:3], sents[n]), add)

            for n in range(4):
                column(n)
            return

        firsts = [
            (
                send(tx1.at[n, 0:4], rx1.at[n, 0:4], right1, "R"),
                send(tx1.at[n, 4:7], rx1.at[n, 4:7], left1, "L"),
            )
            for n in range(4)
        ]
        acc[0] = local(a + 1)
        acc[1] = local(a - 1)
        acc[2] = local(a)

        def column(n):
            slot, sent = line.slot(), []

            def add():
                acc[2, n] += wide(rx2[0, n]) + wide(rx2[1, n])
                line.cost(0.15)
                then[n]()

            def sent_both():
                if len(sent) == 2:
                    after(line.together(slot, rx2.at[:, n], sent), add)

            def to_right():
                acc[0, n, 0:64] += wide(rx1[n, 0:4])
                tx2[0, n] = tiles(acc[0, n])
                line.cost(0.1)
                sent.append(send(tx2.at[0, n], rx2.at[0, n], right1, "R", slot))
                sent_both()

            def to_left():
                acc[1, n, 64:112] += wide(rx1[n, 4:7])
                tx2[1, n] = tiles(acc[1, n])
                line.cost(0.1)
                sent.append(send(tx2.at[1, n], rx2.at[1, n], left1, "L", slot))
                sent_both()

            after(firsts[n][0], to_right)
            after(firsts[n][1], to_left)

        for n in range(4):
            column(n)

    def spread_cov(p):
        w, acc, rxz, sbuf = WIDTHS[p], buf["acc", p], buf["rxz", p], buf["sbuf", p]
        total = acc[2, 3] + rxz[...].astype(F32).reshape(BLK, w)
        sbuf[pl.ds(block(a, b), 7)] = total.astype(BF16).reshape(7, 16, w)
        line.cost(0.2)

        def part(i, j, k):
            if i is None:
                return sbuf.at[pl.ds(0, 7 * k)]
            n = block(i, j)
            if k is None:
                return sbuf.at[pl.ds(n, 7)]
            return sbuf.at[pl.ds(n, 4)] if k == 0 else sbuf.at[pl.ds(n + 4, 3)]

        gather(part, lambda: begin_steps(p), p in NEAR1, p in FAST)

    dst = lax.broadcasted_iota(jnp.int32, (2 * PAD, BLK), 0)
    src = lax.broadcasted_iota(jnp.int32, (2 * PAD, BLK), 1)
    row = dst & 31
    pick = jnp.where((src == 56 * zh + (dst >> 5) * ROWS + row) & (row < ROWS), 1.0, 0.0).astype(BF16)
    raws, squares, seen = {}, [], []

    def rows(p, k):
        return buf["sbuf", p][16 * k : 16 * k + 16].reshape(256, WIDTHS[p])

    def begin_steps(p):
        raws[p] = dot(pick, buf["sbuf", p][pl.ds(block(a, b), 7)].reshape(BLK, WIDTHS[p]))
        square = jnp.zeros((1, WIDTHS[p]), F32)
        for k in range(7):
            value = rows(p, k)
            partial = dot_nt(raws[p].astype(BF16), value)
            ptx[0, k] = ptx[0, k] + partial if seen else partial
            if len(seen) + 1 == len(WIDTHS):
                exchange(0, k)
            value = value.astype(F32)
            square += jnp.sum(value * value, axis=0, keepdims=True)
        squares.append(jnp.sum(square, axis=1, keepdims=True))
        seen.append(p)
        line.cost(0.8)

    copies = [{} for _ in range(4)]

    def exchange(n, k):
        if k in GROUPS:
            group = pl.ds(k - GROUPS[k] + 1, GROUPS[k])
            copies[n][k - GROUPS[k] + 1] = send(ptx.at[n, group], prx.at[n, group], other, "core")

    begin(0)
    line.run()

    qtx[...] = jnp.broadcast_to(sum(squares), (8, 128))
    squared = send(qtx, qrx, other, "core")

    def span(k, count):
        return jnp.concatenate(
            [buf["sbuf", p][16 * k : 16 * (k + count)].reshape(256 * count, w) for p, w in enumerate(WIDTHS)], axis=1
        )

    def second_half(n):
        result = jnp.zeros((2 * PAD, H), F32)
        for last, count in GROUPS.items():
            k = last - count + 1
            copies[n][k][0]()
            inner = [(ptx[n, i] + prx[n, i]).astype(BF16) for i in range(k, last + 1)]
            result += dot(jnp.concatenate(inner, axis=1), span(k, count))
        return result

    def apply(vector, n):
        low = vector.astype(BF16)
        for k in range(7):
            ptx[n, k] = dot_nt(low, span(k, 1))
            exchange(n, k)
        return second_half(n)

    raw = jnp.concatenate([raws[p] for p in PARTS], axis=1)
    once = second_half(0)
    squared[0]()
    scale = 2.0 * jnp.sqrt((qtx[0:1, 0:1] + qrx[0:1, 0:1]) / W + 1e-06)
    inverse = 1.0 / scale
    square_inverse = inverse * inverse
    first = (1.5 * raw - 0.5 * (once * square_inverse)) * inverse
    upper = 1.5 * first - 0.5 * (apply(first, 1) * square_inverse)
    middle = apply(upper, 2) * square_inverse
    cubic = 1.5 * middle - 0.5 * (apply(middle, 3) * square_inverse)
    result = (math.sqrt(W) * (1.5 * first - 0.5 * cubic)).astype(BF16)
    finals = []
    for p, w in enumerate(WIDTHS):
        buf["ofin", p][...] = result[:, STARTS[p] : STARTS[p] + w].reshape(2, PAD, w)
        finals.append(send(buf["ofin", p].at[1 - core], buf["orx", p], other, "core"))
    for p, w in enumerate(WIDTHS):
        ofin, orx = buf["ofin", p], buf["orx", p]
        low, high = slice(STARTS[p], STARTS[p] + w), slice(H + STARTS[p], H + STARTS[p] + w)
        finals[p][0]()

        @pl.when(core == 0)
        def _():
            next_out[0, :, low] = ofin[0, 0:ROWS]
            next_out[0, :, high] = orx[0:ROWS]

        @pl.when(core == 1)
        def _():
            next_out[0, :, high] = ofin[1, 0:ROWS]
            next_out[0, :, low] = orx[0:ROWS]

    line.finish()


def shards(features, pairing, rotation):
    vmem = pl.BlockSpec(memory_space=pltpu.VMEM)
    return pl.pallas_call(
        kernel,
        out_shape=(
            jax.ShapeDtypeStruct((T, W), BF16),
            jax.ShapeDtypeStruct((1, ROWS, W), BF16),
        ),
        in_specs=[vmem] * 3,
        out_specs=(vmem, vmem),
        scratch_shapes=[spec for _, spec in scratch()],
        compiler_params=pltpu.CompilerParams(
            collective_id=0, has_side_effects=True, vmem_limit_bytes=60 * 1024 * 1024
        ),
    )(features, pairing, rotation)


def solution(mesh):
    placed = (P("ckpt", "tok", None), P("ckpt", "tok", None), P("ckpt", "tok", None))
    return jax.shard_map(
        shards,
        mesh=mesh,
        in_specs=placed,
        out_specs=(P("tok", None), P("ckpt", "tok", None)),
        check_vma=False,
    )
```

time: 735 us -> 115 us (0.16)
  waiting for transfers between devices: 341 us -> 0 us
  blocking collectives: 288 us -> 0 us
  Pallas kernels: 0 us -> 112 us
  matrix products: 41.3 us -> 0 us
  local copies, waits for them, and re-layouts: 30.5 us -> 2.5 us
  starting transfers between devices: 15.9 us -> 0 us
  between operations: 14.5 us -> 0.65 us
    all_gather x2 -> x0, waiting for transfers between devices: 298 us -> none  [the longest x1 181 us: shards(): lax.all_gather(rot_rows, 'tok', axis=0, tiled=True)]
    psum x1 -> x0, blocking collectives: 191 us -> none  [normalize(): squares = lax.psum(jnp.sum(own_cov * own_cov), 'tok')]
    pallas_call x0 -> x1, Pallas kernels: none -> 112 us  [shards(): pl.pallas_call(kernel, out_shape=(jax.ShapeDtypeStruct((T, W), BF16), jax...]
    all_to_all x1 -> x0, blocking collectives: 96.3 us -> none  [send_narrow(): lax.all_to_all(right, 'tok', split_axis=0, concat_axis=0, tiled=True)]
    psum x1 -> x0, waiting for transfers between devices: 43.3 us -> none  [shards(): lax.psum(rotated.astype(jnp.float32).astype(jnp.bfloat16), 'ckpt')]
    dot_general x6 -> x0, matrix products: 41.3 us -> none  [the longest x4 31.1 us: apply_once(): return jnp.dot(inner, whole, preferred_element_type=jnp.float32)]
    all_to_all x1 -> x0, starting transfers between devices: 15.8 us -> none  [send_narrow(): lax.all_to_all(left, 'tok', split_axis=0, concat_axis=0, tiled=True)]
    reshape x1 -> x0, local copies, waits for them, and re-layouts: 13.7 us -> none  [block_form(): return pieces.reshape(row_groups, column_groups, row_width, col_width).tr...]
  transfers between devices with their start and end apart: 4 -> 0, of which waited for: 3 -> 0; matrix products, arithmetic and copies ran while one was open for 2% -> 0% of each run, Pallas kernels for 0% -> 0%
where the time goes in v2:
time: 115 us
  Pallas kernels  112 us (97%)
  local copies, waits for them, and re-layouts  2.5 us (2%)
    pallas_call x1, Pallas kernels, shards(): pl.pallas_call(kernel, out_shape=(jax.ShapeDtypeStruct((T, W), BF16), jax...  112 us
    unnamed x4, local copies, waits for them, and re-layouts  2.5 us

profile of v2, /device:TPU:1, one launch (start us, length us, event | category | flops | bytes accessed | tf_op | source)
XLA Modules:
  0.0 115.0 jit_solution(8589035990443266317)
XLA Ops:
  0.6 111.8 %shard_map.50 = (bf16[128,1792]{1,0:T(8,128)(2,1)}, bf16[1,28,1792]{2,1,0:T(8,128)(2,1)}) custom-call(bf16[1,128,1792]{2,1,0:T(8,128)(2,1)} %feat.1, s32[1,1,128]{2,1,0:T(1,128)} %pair.1, bf16[1,28,1792]{2,1,0:T(8,128)(2,1)} %rot.1), custom_call_target="tpu_custom_call" | custom-call | tf_op jit(solution)/shard_map/pallas_call | solution.py:645
  112.5 0.0 copy-start
  112.5 1.9 %copy.7 = bf16[128,1792]{1,0:T(8,128)(2,1)} copy(bf16[128,1792]{1,0:T(8,128)(2,1)} %get-tuple-element.4) | data formatting | bytes 917504
  114.3 0.0 copy-done
  114.3 0.6 copy.8
Async XLA Ops:
  112.5 1.9 %copy-start = (bf16[1,28,1792]{2,1,0:T(8,128)(2,1)S(1)}, bf16[1,28,1792]{2,1,0:T(8,128)(2,1)}, u32[]{:S(2)}) copy-start(bf16[1,28,1792]{2,1,0:T(8,128)(2,1)} %get-tuple-element.5) | copy-start | bytes 301060

commit v3 on v2

--- a/solution.py
+++ b/solution.py
@@ -19,13 +19,14 @@
 WIDTHS = (256, 256, 256, 128)
 STARTS = tuple(sum(WIDTHS[:p]) for p in range(len(WIDTHS)))
 PARTS = range(len(WIDTHS))
-N_SEND, N_RECV = 48, 220
+N_SEND, N_RECV = 32, 215
 NEAR1 = (0, 1, 2, 3)
 GFAST = (0,)
 FAST = (3,)
 
-RATE, CHIP_RATE = 90e3, 600e3
-HOP, CHIP_HOP, FURTHER = 2.4, 1.6, 0.7
+RATE, CHIP_RATE = 84e3, 600e3
+Z_RATE, FAR_RATE = 39e3, 21e3
+HOP, CHIP_HOP, FURTHER = 2.9, 1.6, 0.8
 BACKLOG = 0.3
 GROUPS = {1: 2, 3: 2, 5: 2, 6: 1}
 
@@ -34,7 +35,9 @@
     out = []
     for p, w in enumerate(WIDTHS):
         for name, shape, dtype in (
-            ("rbuf", (64, PAD, w), BF16),
+            ("rbuf", (32, 2 * ROWS, w), BF16),
+            ("rpart", (2, PAD, w), BF16),
+            ("fpart", (2, PAD, w), BF16),
             ("rsend", (PAD, w), BF16),
             ("rotq", (4, 64, w), BF16),
             ("rotr", (4, 64, w), BF16),
@@ -117,8 +120,8 @@
             "L": ("L", RATE, HOP),
             "RL": ("RL", RATE, HOP + FURTHER),
             "core": ("C", CHIP_RATE, CHIP_HOP),
-            "z": ("Z", RATE / 2, HOP + FURTHER),
-            "far": ("Z", RATE / 4, HOP + 3 * FURTHER),
+            "z": ("Z", Z_RATE, HOP + FURTHER),
+            "far": ("Z", FAR_RATE, HOP + 3 * FURTHER),
         }[lane]
         self.now += 0.02
         for name in names:
@@ -266,23 +269,33 @@
             after(move(a, b, None, across1, "RL"), from_across)
         spread(0)
 
+    dst = lax.broadcasted_iota(jnp.int32, (2 * ROWS, 2 * PAD), 0)
+    src = lax.broadcasted_iota(jnp.int32, (2 * ROWS, 2 * PAD), 1)
+    second = (dst >= ROWS).astype(jnp.int32)
+    want = dst - ROWS * second + PAD * (second + core - 2 * core * second)
+    order_rows = jnp.where(src == want, 1.0, 0.0).astype(BF16)
+
+    def compose(p, plane, pieces):
+        value = dot(order_rows, pieces[...].reshape(2 * PAD, WIDTHS[p]))
+        buf["rbuf", p][chip(a, b, plane)] = value.astype(BF16)
+
     swaps, fars = [], []
     for p, w in enumerate(WIDTHS):
-        rbuf, rsend = buf["rbuf", p], buf["rsend", p]
+        rpart, fpart, rsend = buf["rpart", p], buf["fpart", p], buf["rsend", p]
         low = rot[0, :, STARTS[p] : STARTS[p] + w].astype(F32)
         high = rot[0, :, H + STARTS[p] : H + STARTS[p] + w].astype(F32)
         zeros = jnp.zeros((PAD - ROWS, w), BF16)
         rsend[0:ROWS, :] = jnp.where(core == 0, high, low).astype(BF16)
         rsend[ROWS:PAD, :] = zeros
-        swaps.append(send(rsend, rbuf.at[tok], other, "core"))
-        rbuf[tok, 0:ROWS, :] = jnp.where(core == 0, low, high).astype(BF16)
-        rbuf[tok, ROWS:PAD, :] = zeros
+        swaps.append(send(rsend, rpart.at[1], other, "core"))
+        rpart[0, 0:ROWS, :] = jnp.where(core == 0, low, high).astype(BF16)
+        rpart[0, ROWS:PAD, :] = zeros
         slot = line.slot()
         sent = [
-            send(rsend, rbuf.at[tok], far_other, "far", slot),
-            send(rbuf.at[tok], rbuf.at[tok], far, "far", slot),
+            send(rsend, fpart.at[1], far_other, "far", slot),
+            send(rpart.at[0], fpart.at[0], far, "far", slot),
         ]
-        fars.append(line.together(slot, rbuf.at[pl.ds(0, 2)], sent))
+        fars.append(line.together(slot, fpart, sent))
 
     def begin(p):
         rbuf = buf["rbuf", p]
@@ -290,20 +303,24 @@
         def part(plane):
             def of(i, j, k):
                 if i is None:
-                    return rbuf.at[pl.ds(0, 2 * k)]
-                base = chip(i, j, plane) * 2
-                return rbuf.at[pl.ds(base, 2)] if k is None else rbuf.at[base + k]
+                    return rbuf.at[pl.ds(0, k)]
+                n = chip(i, j, plane)
+                if k is None:
+                    return rbuf.at[n]
+                return rbuf.at[n, pl.ds(0, PAD)] if k == 0 else rbuf.at[n, pl.ds(PAD, 2 * ROWS - PAD)]
 
             return of
 
         done = when_all(2 if p else 4, lambda: rotate(p))
 
         def near():
+            compose(p, zh, buf["rpart", p])
             gather(part(zh), done, p in NEAR1, p in GFAST)
             if p == 0:
                 align(done)
 
         def distant():
+            compose(p, 1 - zh, buf["fpart", p])
             gather(part(1 - zh), done, p in NEAR1, p in GFAST)
             if p + 1 in PARTS:
                 begin(p + 1)
@@ -322,9 +339,7 @@
             width = min(384, W - start)
             src = lax.broadcasted_iota(jnp.int32, (width, 256), 0)
             dst = lax.broadcasted_iota(jnp.int32, (width, 256), 1)
-            row = dst & 31
-            want = (224 * g - start) + (dst >> 5) * ROWS + row
-            place = jnp.where((src == want) & (row < ROWS), 1.0, 0.0).astype(BF16)
+            place = jnp.where((src == dst + (224 * g - start)) & (dst < 224), 1.0, 0.0).astype(BF16)
             apad[core, g] = dot(aown[:, start : start + width], place).astype(BF16)
         dst = lax.broadcasted_iota(jnp.int32, (448, 512), 0)
         src = lax.broadcasted_iota(jnp.int32, (448, 512), 1)
@@ -339,20 +354,21 @@
             at[core, 28 * n : 28 * n + 28] = window.astype(BF16).reshape(28, 16, T)
         after(send(apad.at[core], apad.at[core], other, "core"), done)
         after(send(at.at[core], at.at[core], other, "core"), done)
-        line.cost(3.0)
+        line.cost(1.2)
 
     def rotate(p):
         w, racc, rbuf, rotq, rotr = WIDTHS[p], buf["racc", p], buf["rbuf", p], buf["rotq", p], buf["rotr", p]
-        racc[...] = jnp.zeros_like(racc)
-
-        def step(g, carry):
-            left = jnp.concatenate([apad[0, g], apad[1, g]], axis=0)
-            racc[...] += dot(left, rbuf[pl.ds(8 * g, 8)].reshape(8 * PAD, w))
-            return carry
-
-        lax.fori_loop(0, 8, step, 0)
+        for half in range(2):
+            groups = range(4 * half, 4 * half + 4)
+            left = jnp.concatenate([apad[:, g].reshape(2 * T, 256) for g in groups], axis=1)
+            fill = jnp.zeros((256 - 8 * ROWS, w), BF16)
+            right = []
+            for g in groups:
+                right += [rbuf[4 * g : 4 * g + 4].astype(F32).reshape(8 * ROWS, w).astype(BF16), fill]
+            product = dot(left, jnp.concatenate(right, axis=0))
+            racc[...] = racc[...] + product if half else product
         rotq[...] = racc[...].astype(BF16).reshape(4, 64, w)
-        line.cost(w / 300)
+        line.cost(w / 600)
         slot = line.slot()
         sent = [send(rotq.at[m], rotr.at[ck], (m, tok), "z", slot) for m in members]
         after(line.together(slot, rotr.at[pl.ds(0, 3)], sent), lambda: mean(p))
@@ -363,7 +379,7 @@
         for m in members:
             total += rotr[m].astype(F32)
         cons[ck] = (total * 0.25).astype(BF16)
-        line.cost(0.2)
+        line.cost(0.05)
 
         def whole():
             after(send(cons.at[pl.ds(2 * (1 - core), 2)], crx, other, "core"), lambda: store(p))
@@ -387,7 +403,7 @@
             cons_out[:, high] = cons[2:4].reshape(T, w)
             cons_out[:, low] = crx[...].reshape(T, w)
 
-        line.cost(0.1)
+        line.cost(0.03)
 
     def block(i, j):
         px, py = xy(i, j)
@@ -407,7 +423,7 @@
                 sides.append(
                     jnp.concatenate([at[k, pl.ds(block(i, b + j), 7)].reshape(BLK, T) for j in order], axis=0)
                 )
-            line.cost(w / 500)
+            line.cost(w / 1500)
             return dot(jnp.concatenate(sides, axis=1), cvalue).reshape(4, BLK, w)
 
         def tiles(value):
@@ -421,7 +437,7 @@
 
         def final():
             txz[...] = tiles(acc[2, 3])
-            line.cost(0.2)
+            line.cost(0.05)
             after(send(txz, rxz, far, "far"), lambda: spread_cov(p))
 
         direct2 = p in NEAR1
@@ -435,7 +451,7 @@
             acc[2, 3] += wide(rx4[0]) + wide(rx4[1])
             if direct2:
                 acc[2, 3] += wide(rx3[...])
-            line.cost(0.2)
+            line.cost(0.05)
             finals()
 
         finals = when_all(2, final)
@@ -445,7 +461,7 @@
             if not direct2:
                 acc[2, 1, 0:64] += wide(rx3[0:4])
             tx4[0] = tiles(acc[2, 1])
-            line.cost(0.1)
+            line.cost(0.03)
             sent.append(send(tx4.at[0], rx4.at[0], right2, "R", slot))
             last()
 
@@ -453,7 +469,7 @@
             if not direct2:
                 acc[2, 2, 64:112] += wide(rx3[4:7])
             tx4[1] = tiles(acc[2, 2])
-            line.cost(0.1)
+            line.cost(0.03)
             sent.append(send(tx4.at[1], rx4.at[1], left2, "L", slot))
             last()
 
@@ -481,7 +497,7 @@
             def column(n):
                 def add():
                     acc[2, n] += wide(rx1[n]) + wide(rx2[0, n]) + wide(rx2[1, n])
-                    line.cost(0.2)
+                    line.cost(0.05)
                     then[n]()
 
                 after(line.together(slots[n], tx1.at[0:3], sents[n]), add)
@@ -506,7 +522,7 @@
 
             def add():
                 acc[2, n] += wide(rx2[0, n]) + wide(rx2[1, n])
-                line.cost(0.15)
+                line.cost(0.04)
                 then[n]()
 
             def sent_both():
@@ -516,14 +532,14 @@
             def to_right():
                 acc[0, n, 0:64] += wide(rx1[n, 0:4])
                 tx2[0, n] = tiles(acc[0, n])
-                line.cost(0.1)
+                line.cost(0.03)
                 sent.append(send(tx2.at[0, n], rx2.at[0, n], right1, "R", slot))
                 sent_both()
 
             def to_left():
                 acc[1, n, 64:112] += wide(rx1[n, 4:7])
                 tx2[1, n] = tiles(acc[1, n])
-                line.cost(0.1)
+                line.cost(0.03)
                 sent.append(send(tx2.at[1, n], rx2.at[1, n], left1, "L", slot))
                 sent_both()
 
@@ -537,7 +553,7 @@
         w, acc, rxz, sbuf = WIDTHS[p], buf["acc", p], buf["rxz", p], buf["sbuf", p]
         total = acc[2, 3] + rxz[...].astype(F32).reshape(BLK, w)
         sbuf[pl.ds(block(a, b), 7)] = total.astype(BF16).reshape(7, 16, w)
-        line.cost(0.2)
+        line.cost(0.05)
 
         def part(i, j, k):
             if i is None:
@@ -571,7 +587,7 @@
             square += jnp.sum(value * value, axis=0, keepdims=True)
         squares.append(jnp.sum(square, axis=1, keepdims=True))
         seen.append(p)
-        line.cost(0.8)
+        line.cost(0.4)
 
     copies = [{} for _ in range(4)]
 
@@ -640,9 +656,14 @@
     line.finish()
 
 
+def keep(cons, following, cons_out, next_out):
+    cons_out[...] = cons[...]
+    next_out[...] = following[...]
+
+
 def shards(features, pairing, rotation):
     vmem = pl.BlockSpec(memory_space=pltpu.VMEM)
-    return pl.pallas_call(
+    outs = pl.pallas_call(
         kernel,
         out_shape=(
             jax.ShapeDtypeStruct((T, W), BF16),
@@ -655,6 +676,12 @@
             collective_id=0, has_side_effects=True, vmem_limit_bytes=60 * 1024 * 1024
         ),
     )(features, pairing, rotation)
+    return pl.pallas_call(
+        keep,
+        out_shape=tuple(jax.ShapeDtypeStruct(out.shape, out.dtype) for out in outs),
+        in_specs=[vmem] * 2,
+        out_specs=(vmem, vmem),
+    )(*outs)
 
 
 def solution(mesh):

time: 115 us -> 111 us (0.965)
  local copies, waits for them, and re-layouts: 2.5 us -> 0 us
  Pallas kernels: 112 us -> 110 us
    pallas_call x1, Pallas kernels: 112 us -> 108 us  [shards(): pl.pallas_call(kernel, out_shape=(jax.ShapeDtypeStruct((T, W), BF16), jax...]
    unnamed x4 -> x0, local copies, waits for them, and re-layouts: 2.5 us -> none
    pallas_call x0 -> x1, Pallas kernels: none -> 1.87 us  [shards(): pl.pallas_call(keep, out_shape=tuple((jax.ShapeDtypeStruct(out.shape, out...]
where the time goes in v3:
time: 111 us
  Pallas kernels  110 us (99%)
    pallas_call x1, Pallas kernels, shards(): pl.pallas_call(kernel, out_shape=(jax.ShapeDtypeStruct((T, W), BF16), jax...  108 us

profile of v3, /device:TPU:1, one launch (start us, length us, event | category | flops | bytes accessed | tf_op | source)
XLA Modules:
  0.0 110.6 jit_solution(16402983802796329994)
XLA Ops:
  0.6 108.1 %shard_map.50 = (bf16[128,1792]{1,0:T(8,128)(2,1)}, bf16[1,28,1792]{2,1,0:T(8,128)(2,1)}) custom-call(bf16[1,128,1792]{2,1,0:T(8,128)(2,1)} %feat.1, s32[1,1,128]{2,1,0:T(1,128)} %pair.1, bf16[1,28,1792]{2,1,0:T(8,128)(2,1)} %rot.1), custom_call_target="tpu_custom_call" | custom-call | tf_op jit(solution)/shard_map/pallas_call | solution.py:666
  108.7 1.9 %shard_map.51 = (bf16[128,1792]{1,0:T(8,128)(2,1)}, bf16[1,28,1792]{2,1,0:T(8,128)(2,1)}) custom-call(bf16[128,1792]{1,0:T(8,128)(2,1)} %get-tuple-element.4.cons, bf16[1,28,1792]{2,1,0:T(8,128)(2,1)} %get-tuple-element.5.following), custom_call_target="tpu_custom_call" | custom-call | tf_op jit(solution)/shard_map/pallas_call | solution.py:679
